TPU v7x, 256 devices: a whole 4x4x8 slice. The times are simulated.
256 devices in a mesh: grp: 16 (over x_lo, z), inner: 16 (over y, x_hi, core).
Axes of the slice: x: 4 (x_hi: 2, x_lo: 2; x = x_hi * 2 + x_lo), y: 4, z: 8, core: 2. Of those that a mesh axis runs over, the one named last changes fastest.
Arguments:
- signal: bfloat16 [128, 1024, 4096], P('grp', None, 'inner'), may hold values from -6 to 6
- bins: int32 [8], replicated, may hold values from 1 to 512, as said below
- mic_positions: float32 [3, 4096], replicated, may hold values from -1 to 1
- grid_positions: float32 [3, 1024], replicated, may hold values from 1 to 3
Outputs:
- beam_map: float32 [8, 1024], replicated
Inputs may be any that keep to these rules, and one draw needn't show every extreme that they name: The 8 bins are distinct; bin 1 and bin 1024 / 2 are always among them.
All inputs are finite; a program needn't handle non-finite values.
Results may differ from a plain program's by a relative error of at most 0.02.
Values may be sent and summed in bfloat16 or wider, within the bound.
A program may use at most 128 MiB of HBM per device.

v0:
```python
import math
import jax
import jax.numpy as jnp
from jax import lax
from jax.sharding import PartitionSpec as P

SAMPLES = 1024
F = 8
TWO_PI = 2.0 * math.pi
RATE_OVER_SOUND = 51200.0 / 343.0


def dft_table(bins):
    ticks = jnp.arange(SAMPLES, dtype=jnp.int32)
    turns = bins[:, None] * ticks[None, :] % SAMPLES
    angle = turns.astype(jnp.float32) * (TWO_PI / SAMPLES)
    window = 0.5 - 0.5 * jnp.cos(ticks.astype(jnp.float32) * (TWO_PI / SAMPLES))
    factor = math.sqrt(8.0 / (3.0 * SAMPLES))
    real_part = window[None, :] * jnp.cos(angle) * factor
    imag_part = -window[None, :] * jnp.sin(angle) * factor
    return jnp.concatenate([real_part, imag_part], 0).astype(jnp.bfloat16)


def distances(spots, grid):
    delta_x = grid[0][None, :] - spots[0][:, None]
    delta_y = grid[1][None, :] - spots[1][:, None]
    delta_z = grid[2][None, :] - spots[2][:, None]
    return jnp.sqrt(delta_x * delta_x + delta_y * delta_y + delta_z * delta_z) * RATE_OVER_SOUND


def steering(delay, frequency_bin):
    angle = delay * (frequency_bin.astype(jnp.float32) * (TWO_PI / SAMPLES))
    return jnp.concatenate([jnp.cos(angle), -jnp.sin(angle)], 0).astype(jnp.bfloat16)


def shards(signal, bins, mic_positions, grid_positions):
    table = dft_table(bins)
    local = jnp.einsum("kt,stm->skm", table, signal, preferred_element_type=jnp.float32).astype(
        jnp.bfloat16
    )
    snap_dev = local.shape[0]
    mic_cols = local.shape[2]
    local = local.reshape(snap_dev, 2, F, mic_cols)
    grp_size = lax.axis_size("grp")
    grp_index = lax.axis_index("grp")
    inner_index = lax.axis_index("inner")
    total_mics = mic_positions.shape[1]
    snaps = snap_dev * grp_size
    col_pos = lax.dynamic_slice_in_dim(mic_positions, inner_index * mic_cols, mic_cols, 1)
    col_delay = distances(col_pos, grid_positions)
    wide = lax.all_gather(local, "inner", axis=3, tiled=True)
    rows = lax.all_to_all(wide, "grp", split_axis=3, concat_axis=0, tiled=True)
    row_count = rows.shape[3]
    row_ids = grp_index * row_count + jnp.arange(row_count, dtype=jnp.int32)
    row_pos = lax.dynamic_slice_in_dim(mic_positions, grp_index * row_count, row_count, 1)
    col_ids = inner_index * mic_cols + jnp.arange(mic_cols, dtype=jnp.int32)
    row_delay = distances(row_pos, grid_positions)
    piece = lax.all_gather(local, "grp", axis=0, tiled=True)
    real_rows = rows[:, 0]
    imag_rows = rows[:, 1]
    real_cols = piece[:, 0]
    imag_cols = piece[:, 1]
    form = "sfm,sfn->fmn"
    real_sum = jnp.einsum(
        form, real_rows, real_cols, preferred_element_type=jnp.float32
    ) + jnp.einsum(form, imag_rows, imag_cols, preferred_element_type=jnp.float32)
    imag_sum = jnp.einsum(
        form, imag_rows, real_cols, preferred_element_type=jnp.float32
    ) - jnp.einsum(form, real_rows, imag_cols, preferred_element_type=jnp.float32)
    diagonal_mask = row_ids[:, None] == col_ids[None, :]
    partial_value = []
    for index in range(F):
        real_c = jnp.where(diagonal_mask, 0.0, real_sum[index] / snaps)
        imag_c = jnp.where(diagonal_mask, 0.0, imag_sum[index] / snaps)
        block = jnp.concatenate(
            [jnp.concatenate([real_c, -imag_c], 1), jnp.concatenate([imag_c, real_c], 1)], 0
        )
        col_steer = steering(col_delay, bins[index]).astype(jnp.float32)
        row_steer = steering(row_delay, bins[index]).astype(jnp.float32)
        image = jnp.dot(
            block, col_steer, precision=lax.Precision.HIGHEST, preferred_element_type=jnp.float32
        )
        partial_value.append(jnp.sum(row_steer * image, axis=0))
    partial_value = jnp.stack(partial_value, 0)
    total = lax.psum(partial_value, ("grp", "inner"))
    return total * (math.sqrt(snaps) / total_mics)


def solution(mesh):
    in_specs = (P("grp", None, "inner"), P(), P(), P())
    out_specs = P()
    return jax.shard_map(shards, mesh=mesh, in_specs=in_specs, out_specs=out_specs, check_vma=False)
```

profile of v0, /device:TPU:1, one launch (start us, length us, event | category | flops | bytes accessed | tf_op | source)
XLA Modules:
  0.0 348.1 jit_solution(14160871644973293209)
XLA Ops:
  6.6 0.9 multiply_convert_fusion.1
  7.5 3.5 fusion
  10.9 0.0 all-gather.3.cloned.1.call-update
  11.0 0.0 all-gather.5.cloned.1.call-start
  11.0 0.7 all-gather.5.cloned.1.call-update
  11.7 51.2 %all-gather.3.cloned.1.call-done = bf16[8,2,8,4096]{3,2,1,0:T(8,128)(2,1)} async-done(((bf16[8,2,8,256]{3,2,1,0:T(8,128)(2,1)}), bf16[8,2,8,4096]{3,2,1,0:T(8,128)(2,1)}) %all-gather.3.cloned.1.call-update) | async-done | bytes 1048592 | tf_op jit(solution)/shard_map/all_gather | solution.py:51
  62.9 32.9 %copy.11 = bf16[8,2,8,4096]{2,1,0,3:T(2,128)(2,1)} copy(bf16[8,2,8,4096]{3,2,1,0:T(8,128)(2,1)} %all-gather.3.cloned.1.call-done) | data formatting | bytes 2097152 | tf_op jit(solution)/shard_map/all_gather | solution.py:51
  95.8 20.6 %reshape.88 = bf16[16,2,16384]{2,1,0:T(2,128)(2,1)} reshape(bf16[4096,8,2,8]{3,2,1,0:T(2,128)(2,1)} %bitcast.129) | data formatting | bytes 2097152
  116.5 7.0 %all-to-all-start = ((bf16[16,2,16384]{2,1,0:T(2,128)(2,1)}), bf16[16,2,16384]{2,1,0:T(2,128)(2,1)S(1)}, u32[]{:S(2)}, u32[]{:S(2)}) async-start(bf16[16,2,16384]{2,1,0:T(2,128)(2,1)} %reshape.88), calls=%async_computation | async-start | bytes 2097152 | tf_op jit(solution)/shard_map/all_to_all | solution.py:52
  123.5 0.0 copy-done
  123.5 0.7 fusion.139
  129.3 0.9 constant_dynamic-slice_fusion.1
  130.2 66.2 %cosine_convert_fusion = (bf16[256,1024]{1,0:T(8,128)(2,1)}, bf16[256,1024]{1,0:T(8,128)(2,1)S(1)}, bf16[256,1024]{1,0:T(8,128)(2,1)}, bf16[256,1024]{1,0:T(8,12...) fusion(f32[]{:T(128)} %bitcast.49, ...), kind=kLoop, calls=%fused_computation.109 | loop fusion | flops 20971520 | bytes 16795680 | tf_op jit(solution)/shard_map/convert
  196.4 0.0 all-gather.5.cloned.1.call-done
  196.5 1.3 fusion.137
  197.7 0.4 copy.16
  198.2 0.4 copy.15
  198.6 0.0 all-to-all-done
  198.6 20.8 %reshape.89 = bf16[4096,8,2,8]{3,2,1,0:T(2,128)(2,1)} reshape(bf16[16,2,16384]{2,1,0:T(2,128)(2,1)S(1)} %all-to-all-done) | data formatting | bytes 2097152
  219.4 24.9 %copy.12 = bf16[8,2,8,16,256]{4,0,3,2,1:T(8,128)(2,1)S(1)} copy(bf16[8,2,8,16,256]{2,1,0,4,3:T(2,128)(2,1)} %bitcast.130) | data formatting | bytes 2097152 | tf_op jit(solution)/shard_map/all_to_all | solution.py:52
  244.3 0.4 fusion.83
  244.7 0.4 fusion.85
  245.1 0.4 convolution_add_fusion
  245.6 0.4 convolution_subtract_fusion
  246.0 0.0 copy-start.29
  246.0 0.0 copy-start.30
  246.0 0.0 copy-start.31
  246.0 0.0 copy-start.32
  246.1 0.8 fusion.129
  246.9 0.2 copy-done.29
  247.1 0.2 copy-done.30
  247.2 0.2 copy-done.31
  247.4 0.2 copy-done.32
  247.5 1.9 multiply_reduce_fusion.1
  249.5 0.0 copy-done.25
  249.5 0.0 copy-done.26
  249.5 0.0 copy-done.27
  249.5 0.0 copy-done.28
  249.5 0.0 copy-start.21
  249.5 0.0 copy-start.22
  249.6 0.0 copy-start.23
  249.6 0.0 copy-start.24
  249.6 1.9 multiply_reduce_fusion.2
  251.5 0.0 copy-done.21
  251.5 0.0 copy-done.22
  251.5 0.0 copy-done.23
  251.6 0.0 copy-done.24
  251.6 0.0 copy-start.17
  251.6 0.0 copy-start.18
  251.6 0.0 copy-start.19
  251.6 0.0 copy-start.20
  251.6 1.9 multiply_reduce_fusion.3
  253.6 0.0 copy-done.17
  253.6 0.0 copy-done.18
  253.6 0.0 copy-done.19
  253.6 0.0 copy-done.20
  253.6 1.9 multiply_reduce_fusion.4
  255.7 1.9 multiply_reduce_fusion.5
  257.7 2.2 multiply_reduce_fusion.6
  260.0 1.9 multiply_reduce_fusion
  261.9 1.9 multiply_reduce_fusion.7
  263.9 0.1 stack.35
  263.9 76.7 %psum.7 = f32[8,1024]{1,0:T(8,128)S(1)} all-reduce(f32[8,1024]{1,0:T(8,128)S(1)} %stack.35), channel_id=1, replica_groups=mesh['grp'=16,'inner'=16] {'grp','inner'}, use_global_device_ids=true, to_apply=%region_8.9 | all-reduce | flops 8192 | bytes 65536 | tf_op jit(solution)/shard_map/psum | solution.py:85
  340.6 0.6 broadcast_multiply_fusion
  (41 shorter events, 0.1 us)
Async XLA Ops:
  6.5 56.4 %all-gather.3.cloned.1.call-start = ((), (), s32[]{:S(2)}) async-start(), calls=%async_computation.1 | async-start | bytes 1114112 | tf_op jit(solution)/shard_map/all_gather | solution.py:51
  11.0 185.5 %all-gather.5.cloned.1.call-start = ((), (), s32[]{:S(2)}) async-start(), calls=%async_computation.2 | async-start | bytes 1114112 | tf_op jit(solution)/shard_map/all_gather | solution.py:58
  116.5 7.0 %copy-start = (s32[8]{0:T(128)S(1)}, s32[8]{0:T(128)}, u32[]{:S(2)}) copy-start(s32[8]{0:T(128)} %param.5) | copy-start | bytes 100
  116.5 13.7 %copy-start.1 = (f32[3,1024]{1,0:T(4,128)S(1)}, f32[3,1024]{1,0:T(4,128)}, u32[]{:S(2)}) copy-start(f32[3,1024]{1,0:T(4,128)} %param.7) | copy-start | bytes 36868
  116.5 82.2 %all-to-all-start = ((bf16[16,2,16384]{2,1,0:T(2,128)(2,1)}), bf16[16,2,16384]{2,1,0:T(2,128)(2,1)S(1)}, u32[]{:S(2)}, u32[]{:S(2)}) async-start(bf16[16,2,16384]{2,1,0:T(2,128)(2,1)} %reshape.88), calls=%async_computation | async-start | bytes 2097152 | tf_op jit(solution)/shard_map/all_to_all | solution.py:52
  246.0 1.0 copy-start.29
  246.0 1.2 copy-start.30
  246.0 1.3 copy-start.31
  246.0 1.5 copy-start.32
  247.5 2.0 copy-start.25
  247.5 2.0 copy-start.26
  247.5 2.0 copy-start.27
  247.5 2.0 copy-start.28
  249.5 2.0 copy-start.21
  249.5 2.0 copy-start.22
  249.6 2.0 copy-start.23
  249.6 2.0 copy-start.24
  251.6 2.0 copy-start.17
  251.6 2.0 copy-start.18
  251.6 2.0 copy-start.19
  251.6 2.0 copy-start.20
  253.6 2.0 copy-start.13
  253.6 2.0 copy-start.14
  253.6 2.0 copy-start.15
  253.6 2.0 copy-start.16
  255.6 2.0 copy-start.9
  255.6 2.0 copy-start.10
  255.6 2.0 copy-start.11
  255.6 2.0 copy-start.12
  257.6 2.2 copy-start.5
  257.7 2.2 copy-start.6
  257.7 2.2 copy-start.7
  257.7 2.2 copy-start.8
  259.9 2.0 copy-start.2
  259.9 2.0 copy-start.3
  259.9 2.0 copy-start.4
Sparse Core Ops, SparseCore 0:
  11.1 51.7 all-gather.2
  64.7 57.6 all-gather.4
where the time goes:
time: 353 us; the launch traced here: 348 us
  local copies, waits for them, and re-layouts  104 us (29%)
  blocking collectives  76.7 us (22%)
  other arithmetic  68.6 us (19%)
  waiting for transfers between devices  51.9 us (15%)
  matrix products  20.9 us (6%)
  between operations  19.1 us (5%)
  starting transfers between devices  7.02 us (2%)
    psum x1, blocking collectives, shards(): total = lax.psum(partial_value, ('grp', 'inner'))  76.7 us
    another operation x2, other arithmetic  67.1 us
    all_gather x1, waiting for transfers between devices, shards(): wide = lax.all_gather(local, 'inner', axis=3, tiled=True)  51.2 us
    unnamed x70, local copies, waits for them, and re-layouts  43 us
    all_gather x1, local copies, waits for them, and re-layouts, shards(): wide = lax.all_gather(local, 'inner', axis=3, tiled=True)  32.9 us
    all_to_all x1, local copies, waits for them, and re-layouts, shards(): rows = lax.all_to_all(wide, 'grp', split_axis=3, concat_axis=0, tiled=True)  24.9 us
    dot_general x8, matrix products, shards(): jnp.dot(block, col_steer, precision=lax.Precision.HIGHEST, preferred_elem...  15.8 us
  transfers between devices with their start and end apart: 3, of which 1 were waited for; matrix products, arithmetic and copies ran while one was open for 35% of the time, Pallas kernels for 0%

commit v1 on v0

--- a/solution.py
+++ b/solution.py
@@ -82,7 +82,12 @@
         )
         partial_value.append(jnp.sum(row_steer * image, axis=0))
     partial_value = jnp.stack(partial_value, 0)
-    total = lax.psum(partial_value, ("grp", "inner"))
+
+    def balance_the_roots(m):
+        f_next = jnp.sum(jax.lax.all_gather(m, ("grp", "inner")), 0)
+        return f_next
+
+    total = balance_the_roots(partial_value)
     return total * (math.sqrt(snaps) / total_mics)
 
 

time: 353 us -> 700 us (1.98)
  waiting for transfers between devices: 51.9 us -> 471 us
  blocking collectives: 76.7 us -> 0 us
    all_gather x0 -> x1, waiting for transfers between devices: none -> 419 us  [balance_the_roots(): f_next = jnp.sum(jax.lax.all_gather(m, ('grp', 'inner')), 0)]
    psum x1 -> x0, blocking collectives: 76.7 us -> none  [shards(): total = lax.psum(partial_value, ('grp', 'inner'))]
  transfers between devices with their start and end apart: 3 -> 4, of which waited for: 1 -> 2; matrix products, arithmetic and copies ran while one was open for 35% -> 18% of each run, Pallas kernels for 0% -> 0%
where the time goes in v1:
time: 700 us; the launch traced here: 695 us
  waiting for transfers between devices  471 us (67%)
  local copies, waits for them, and re-layouts  104 us (15%)
  other arithmetic  72.6 us (10%)
  matrix products  20.9 us (3%)
  between operations  18.7 us (3%)
  starting transfers between devices  7.07 us (1%)
    all_gather x1, waiting for transfers between devices, balance_the_roots(): f_next = jnp.sum(jax.lax.all_gather(m, ('grp', 'inner')), 0)  419 us
    another operation x2, other arithmetic  67.1 us
    all_gather x1, waiting for transfers between devices, shards(): wide = lax.all_gather(local, 'inner', axis=3, tiled=True)  51.2 us
    unnamed x70, local copies, waits for them, and re-layouts  43 us
    all_gather x1, local copies, waits for them, and re-layouts, shards(): wide = lax.all_gather(local, 'inner', axis=3, tiled=True)  32.9 us
    all_to_all x1, local copies, waits for them, and re-layouts, shards(): rows = lax.all_to_all(wide, 'grp', split_axis=3, concat_axis=0, tiled=True)  24.9 us
    dot_general x8, matrix products, shards(): jnp.dot(block, col_steer, precision=lax.Precision.HIGHEST, preferred_elem...  15.8 us
  transfers between devices with their start and end apart: 4, of which 2 were waited for; matrix products, arithmetic and copies ran while one was open for 18% of the time, Pallas kernels for 0%

profile of v1, /device:TPU:1, one launch (start us, length us, event | category | flops | bytes accessed | tf_op | source)
XLA Modules:
  0.0 694.8 jit_solution(10848533065960447674)
XLA Ops:
  6.5 0.0 all-gather.5.cloned.1.call-start
  6.6 0.9 multiply_convert_fusion.1
  7.5 3.5 fusion
  10.9 0.0 all-gather.5.cloned.1.call-update
  11.0 0.0 all-gather.7.cloned.1.call-start
  11.0 0.7 all-gather.7.cloned.1.call-update
  11.7 51.2 %all-gather.5.cloned.1.call-done = bf16[8,2,8,4096]{3,2,1,0:T(8,128)(2,1)} async-done(((bf16[8,2,8,256]{3,2,1,0:T(8,128)(2,1)}), bf16[8,2,8,4096]{3,2,1,0:T(8,128)(2,1)}) %all-gather.5.cloned.1.call-update) | async-done | bytes 1048592 | tf_op jit(solution)/shard_map/all_gather | solution.py:51
  62.9 32.9 %copy.15 = bf16[8,2,8,4096]{2,1,0,3:T(2,128)(2,1)} copy(bf16[8,2,8,4096]{3,2,1,0:T(8,128)(2,1)} %all-gather.5.cloned.1.call-done) | data formatting | bytes 2097152 | tf_op jit(solution)/shard_map/all_gather | solution.py:51
  95.8 20.6 %reshape.89 = bf16[16,2,16384]{2,1,0:T(2,128)(2,1)} reshape(bf16[4096,8,2,8]{3,2,1,0:T(2,128)(2,1)} %bitcast.131) | data formatting | bytes 2097152
  116.5 7.0 %all-to-all-start = ((bf16[16,2,16384]{2,1,0:T(2,128)(2,1)}), bf16[16,2,16384]{2,1,0:T(2,128)(2,1)S(1)}, u32[]{:S(2)}, u32[]{:S(2)}) async-start(bf16[16,2,16384]{2,1,0:T(2,128)(2,1)} %reshape.89), calls=%async_computation | async-start | bytes 2097152 | tf_op jit(solution)/shard_map/all_to_all | solution.py:52
  123.5 0.0 all-gather.9.cloned.1.call-start
  123.5 0.0 copy-done
  123.5 0.7 fusion.139
  129.2 0.9 constant_dynamic-slice_fusion.1
  130.1 0.0 copy-done.1
  130.1 66.3 %cosine_convert_fusion = (bf16[256,1024]{1,0:T(8,128)(2,1)}, bf16[256,1024]{1,0:T(8,128)(2,1)S(1)}, bf16[256,1024]{1,0:T(8,128)(2,1)}, bf16[256,1024]{1,0:T(8,12...) fusion(f32[]{:T(128)} %bitcast.49, ...), kind=kLoop, calls=%fused_computation.110 | loop fusion | flops 20971520 | bytes 16795680 | tf_op jit(solution)/shard_map/convert
  196.4 0.0 all-gather.7.cloned.1.call-done
  196.4 1.3 fusion.137
  197.7 0.4 copy.20
  198.2 0.4 copy.19
  198.6 0.0 all-to-all-done
  198.6 20.8 %reshape.90 = bf16[4096,8,2,8]{3,2,1,0:T(2,128)(2,1)} reshape(bf16[16,2,16384]{2,1,0:T(2,128)(2,1)S(1)} %all-to-all-done) | data formatting | bytes 2097152
  219.4 24.9 %copy.16 = bf16[8,2,8,16,256]{4,0,3,2,1:T(8,128)(2,1)S(1)} copy(bf16[8,2,8,16,256]{2,1,0,4,3:T(2,128)(2,1)} %bitcast.132) | data formatting | bytes 2097152 | tf_op jit(solution)/shard_map/all_to_all | solution.py:52
  244.3 0.4 fusion.83
  244.7 0.4 fusion.85
  245.1 0.4 convolution_add_fusion
  245.6 0.4 convolution_subtract_fusion
  246.0 0.0 copy-start.29
  246.0 0.0 copy-start.30
  246.0 0.0 copy-start.31
  246.0 0.8 fusion.129
  246.9 0.2 copy-done.29
  247.0 0.2 copy-done.30
  247.2 0.2 copy-done.31
  247.4 0.2 copy-done.32
  247.5 1.9 multiply_reduce_fusion.1
  249.6 1.9 multiply_reduce_fusion.2
  251.5 0.0 copy-done.21
  251.5 0.0 copy-done.22
  251.5 0.0 copy-done.23
  251.5 0.0 copy-done.24
  251.6 0.0 copy-start.17
  251.6 0.0 copy-start.18
  251.6 0.0 copy-start.19
  251.6 0.0 copy-start.20
  251.6 1.9 multiply_reduce_fusion.3
  253.6 1.9 multiply_reduce_fusion.4
  255.6 0.0 copy-done.13
  255.6 0.0 copy-done.14
  255.6 0.0 copy-done.15
  255.6 0.0 copy-done.16
  255.6 0.0 copy-start.9
  255.6 0.0 copy-start.10
  255.6 0.0 copy-start.11
  255.6 0.0 copy-start.12
  255.6 1.9 multiply_reduce_fusion.5
  257.7 2.2 multiply_reduce_fusion.6
  259.9 1.9 multiply_reduce_fusion
  261.9 1.9 multiply_reduce_fusion.7
  263.8 0.7 stack.35
  264.5 0.0 all-gather.9.cloned.1.call-update
  264.5 419.2 %all-gather.9.cloned.1.call-done = f32[2048,1024]{1,0:T(8,128)} async-done(((f32[8,1024]{1,0:T(8,128)}), f32[2048,1024]{1,0:T(8,128)}) %all-gather.9.cloned.1.call-update) | async-done | bytes 8388624 | tf_op jit(solution)/shard_map/all_gather | solution.py:87
  683.8 3.9 bitcast_reduce_fusion
  687.7 0.6 broadcast_multiply_fusion
  (44 shorter events, 0.1 us)
Async XLA Ops:
  6.5 56.4 %all-gather.5.cloned.1.call-start = ((), (), s32[]{:S(2)}) async-start(), calls=%async_computation.1 | async-start | bytes 1114112 | tf_op jit(solution)/shard_map/all_gather | solution.py:51
  11.0 185.5 %all-gather.7.cloned.1.call-start = ((), (), s32[]{:S(2)}) async-start(), calls=%async_computation.2 | async-start | bytes 1114112 | tf_op jit(solution)/shard_map/all_gather | solution.py:58
  116.5 7.1 %copy-start = (s32[8]{0:T(128)S(1)}, s32[8]{0:T(128)}, u32[]{:S(2)}) copy-start(s32[8]{0:T(128)} %param.5) | copy-start | bytes 100
  116.5 13.7 %copy-start.1 = (f32[3,1024]{1,0:T(4,128)S(1)}, f32[3,1024]{1,0:T(4,128)}, u32[]{:S(2)}) copy-start(f32[3,1024]{1,0:T(4,128)} %param.7) | copy-start | bytes 36868
  116.5 82.1 %all-to-all-start = ((bf16[16,2,16384]{2,1,0:T(2,128)(2,1)}), bf16[16,2,16384]{2,1,0:T(2,128)(2,1)S(1)}, u32[]{:S(2)}, u32[]{:S(2)}) async-start(bf16[16,2,16384]{2,1,0:T(2,128)(2,1)} %reshape.89), calls=%async_computation | async-start | bytes 2097152 | tf_op jit(solution)/shard_map/all_to_all | solution.py:52
  123.5 560.3 %all-gather.9.cloned.1.call-start = ((), (), s32[]{:S(2)}) async-start(), calls=%async_computation.3 | async-start | bytes 8421376 | tf_op jit(solution)/shard_map/all_gather | solution.py:87
  246.0 1.0 copy-start.29
  246.0 1.2 copy-start.30
  246.0 1.3 copy-start.31
  246.0 1.5 copy-start.32
  247.5 2.0 copy-start.25
  247.5 2.0 copy-start.26
  247.5 2.0 copy-start.27
  247.5 2.0 copy-start.28
  249.5 2.0 copy-start.21
  249.5 2.0 copy-start.22
  249.5 2.0 copy-start.23
  249.5 2.0 copy-start.24
  251.6 2.0 copy-start.17
  251.6 2.0 copy-start.18
  251.6 2.0 copy-start.19
  251.6 2.0 copy-start.20
  253.6 2.0 copy-start.13
  253.6 2.0 copy-start.14
  253.6 2.0 copy-start.15
  253.6 2.0 copy-start.16
  255.6 2.0 copy-start.9
  255.6 2.0 copy-start.10
  255.6 2.0 copy-start.11
  255.6 2.0 copy-start.12
  257.6 2.2 copy-start.5
  257.6 2.2 copy-start.6
  257.7 2.2 copy-start.7
  257.7 2.2 copy-start.8
  259.9 2.0 copy-start.2
  259.9 2.0 copy-start.3
  259.9 2.0 copy-start.4
Sparse Core Ops, SparseCore 0:
  11.1 51.7 all-gather.4
  64.7 57.6 all-gather.6
  264.7 419.0 all-gather.8
